TPU v7x, 32 devices: a whole 2x2x4 slice. The times are simulated.
32 devices in a mesh: mesh: 8 (over y, x, core), state: 4 (over z).
Axes of the slice: x: 2, y: 2, z: 4, core: 2. Of those that a mesh axis runs over, the one named last changes fastest.
Arguments:
- kern_blocks: bfloat16 [192, 16, 128, 128], P('mesh'), may hold values from 4.296875e-06 to 0.13744531
- kern_cols: int32 [192, 16], P('mesh'), may hold values from 0 to 191, as said below
- state_kernel: bfloat16 [512, 512], replicated, may hold values from 0 to 0.61, as said below
- start_v: float32 [24576, 512], P('mesh', 'state'), may hold values from 0.5 to 5
- mu: float32 [24576, 512], P(('mesh', 'state')), may hold values from 0.2 to 2
- nu: float32 [24576, 512], P('mesh', 'state'), may hold values from 0.2 to 2
Outputs:
- potential_u: float32 [24576, 512], P(('mesh', 'state'))
- potential_v: float32 [24576, 512], P('mesh', 'state')
Inputs may be any that keep to these rules, and one draw needn't show every extreme that they name: `kern_cols`: each block row names 16 different block columns, its own block among them. The block rows held by index d of mesh (rows d * 24 to (d + 1) * 24 - 1) refer, among the blocks of index d - 1 and d + 1 (wrapping around 8), only to the last 6 blocks of d - 1 and the first 6 blocks of d + 1, and to all of them; among the blocks of every other index, to at most 2 distinct blocks, and to exactly 2 of index d + 2. How many other indices they reach differs from index to index. `state_kernel`: each row has a positive diagonal entry.
All inputs are finite; a program needn't handle non-finite values.
Results may differ from a plain program's by a relative error of at most 0.0033.
Values may be sent and summed in bfloat16 or wider, within the bound.
No kernel may reach another device: no remote copies, remote signals or barrier semaphores. Data moves between devices by JAX's collectives and lax.ppermute only.
A program may use at most 192 MiB of HBM per device.

v0:
```python
import jax
import jax.numpy as jnp
from jax import lax
from jax.sharding import PartitionSpec as P

CAP_FAR = 2
ITERS = 2
CAP_NEAR = 6


def padded_2(cells, sides, width):
    for axis, dim in sides:
        count = lax.axis_size(axis)
        head = lax.slice_in_dim(cells, 0, width, axis=dim)
        tail = lax.slice_in_dim(cells, cells.shape[dim] - width, cells.shape[dim], axis=dim)
        cells = jnp.concatenate(
            [
                lax.ppermute(tail, axis, [(i, (i + 1) % count) for i in range(count)]),
                cells,
                lax.ppermute(head, axis, [((i + 1) % count, i) for i in range(count)]),
            ],
            axis=dim,
        )
    return cells


def shifted(value, axis, steps):
    count = lax.axis_size(axis)
    pairs = [(source, (source + steps) % count) for source in range(count)]
    return lax.ppermute(value, axis, pairs)


def request_plan(owners, places, remote, peer_count, block_rows, width):
    peer_ids = jnp.arange(peer_count, dtype=jnp.int32)
    place_ids = jnp.arange(block_rows, dtype=jnp.int32)
    matches = (
        remote[:, None, None]
        & (owners[:, None, None] == peer_ids[None, :, None])
        & (places[:, None, None] == place_ids[None, None, :])
    )
    matches = matches.astype(jnp.int32)
    needed = jnp.max(matches, axis=0)
    ranking = jnp.cumsum(needed, axis=1) - needed
    ref_slots = jnp.sum(matches * ranking[None, :, :], axis=(1, 2))
    slot_ids = jnp.arange(width, dtype=jnp.int32)
    selected = needed[:, :, None] * (ranking[:, :, None] == slot_ids[None, None, :]).astype(
        jnp.int32
    )
    requests = jnp.sum(selected * place_ids[None, :, None], axis=1)
    return (ref_slots, requests)


def rounded_sum(values):
    return lax.optimization_barrier(values.astype(jnp.bfloat16)).astype(jnp.float32)


def per_device(kern_blocks, kern_cols, state_kernel, start_v, mu, nu):
    block_rows, degree, block_size, _ = kern_blocks.shape
    local_rows, state_cols = start_v.shape
    peer_count = lax.axis_size("mesh")
    state_count = lax.axis_size("state")
    my_index = lax.axis_index("mesh")
    left_index = (my_index + peer_count - 1) % peer_count
    right_index = (my_index + 1) % peer_count
    flat_cols = kern_cols.reshape(-1)
    owners = flat_cols // block_rows
    places = flat_cols % block_rows
    near_width = CAP_NEAR
    far_base = block_rows + 2 * near_width
    remote = (owners != my_index) & (owners != left_index) & (owners != right_index)
    ref_slots, requests = request_plan(owners, places, remote, peer_count, block_rows, CAP_FAR)
    asked = lax.all_to_all(requests, "mesh", split_axis=0, concat_axis=0, tiled=True)
    near_source = jnp.where(
        owners == left_index,
        places - (block_rows - near_width),
        jnp.where(owners == right_index, near_width + block_rows + places, near_width + places),
    )
    sources = jnp.where(remote, far_base + owners * CAP_FAR + ref_slots, near_source)
    table_size = far_base + peer_count * CAP_FAR
    flat_asked = asked.reshape(-1)
    values = start_v
    potential_u = mu
    for sweep in range(ITERS):
        rounded_v = values.astype(jnp.bfloat16)
        blocks = rounded_v.reshape(block_rows, block_size, state_cols)
        padded = padded_2(rounded_v, (("mesh", 0),), near_width * block_size)
        incoming = lax.all_to_all(blocks[asked], "mesh", split_axis=0, concat_axis=0, tiled=True)
        table = jnp.concatenate(
            [
                padded.reshape(-1, block_size, state_cols),
                incoming.reshape(-1, block_size, state_cols),
            ],
            axis=0,
        )
        picked = table[sources].reshape(block_rows, degree, block_size, state_cols)
        applied = jnp.einsum(
            "rkab,rkbc->rac", kern_blocks, picked, preferred_element_type=jnp.float32
        )
        pieces = applied.astype(jnp.bfloat16).reshape(
            state_count, local_rows // state_count, state_cols
        )
        mixed = jnp.einsum(
            "xrl,jl->xrj",
            lax.all_to_all(pieces, "state", split_axis=0, concat_axis=2, tiled=True),
            state_kernel,
            preferred_element_type=jnp.float32,
        )
        potential_u = mu / mixed[0]
        back_rows = jnp.dot(
            potential_u.astype(jnp.bfloat16), state_kernel, preferred_element_type=jnp.float32
        ).astype(jnp.bfloat16)
        returned = lax.all_to_all(back_rows, "state", split_axis=1, concat_axis=0, tiled=True)
        returned = returned.reshape(block_rows, block_size, state_cols)
        spread = jnp.einsum(
            "rkab,rac->rkbc", kern_blocks, returned, preferred_element_type=jnp.float32
        )
        contrib_table = jax.ops.segment_sum(
            spread.reshape(-1, block_size, state_cols), sources, num_segments=table_size
        )
        own_part = rounded_sum(contrib_table[near_width : near_width + block_rows])
        to_left = contrib_table[:near_width].astype(jnp.bfloat16)
        to_right = contrib_table[near_width + block_rows : far_base].astype(jnp.bfloat16)
        from_right = shifted(to_left, "mesh", -1)
        from_left = shifted(to_right, "mesh", 1)
        outgoing = (
            contrib_table[far_base:]
            .reshape(peer_count, CAP_FAR, block_size, state_cols)
            .astype(jnp.bfloat16)
        )
        arriving = lax.all_to_all(outgoing, "mesh", split_axis=0, concat_axis=0, tiled=True)
        arriving = arriving.reshape(-1, block_size, state_cols).astype(jnp.float32)
        totals = own_part + jax.ops.segment_sum(arriving, flat_asked, num_segments=block_rows)
        totals = totals.at[:near_width].add(from_left.astype(jnp.float32))
        totals = totals.at[block_rows - near_width :].add(from_right.astype(jnp.float32))
        values = nu / totals.reshape(local_rows, state_cols)
    return (potential_u, values)


def solution(mesh):
    placed = (
        P("mesh", None, None, None),
        P("mesh", None),
        P(),
        P("mesh", "state"),
        P(("mesh", "state"), None),
        P("mesh", "state"),
    )
    return jax.shard_map(
        per_device,
        mesh=mesh,
        in_specs=placed,
        out_specs=(P(("mesh", "state"), None), P("mesh", "state")),
        check_vma=False,
    )
```

profile of v0, /device:TPU:0, one launch (start us, length us, event | category | flops | bytes accessed | tf_op | source)
XLA Modules:
  0.0 483.5 jit_solution(15671120138899974268)
XLA Ops:
  3.9 5.2 %all-to-all-start = ((s32[8,1,2]{2,1,0:T(1,128)}), s32[8,1,2]{2,1,0:T(1,128)S(1)}, u32[]{:S(2)}, u32[]{:S(2)}) async-start(s32[8,1,2]{2,1,0:T(1,128)} %copy.49), calls=%async_computation | async-start | bytes 8192 | tf_op jit(solution)/shard_map/all_to_all | solution.py:72
  11.2 2.2 collective-permute-start.1
  15.5 3.5 all-to-all-start.1
  19.1 9.5 %all-to-all-done.1 = bf16[8,2,128,128]{3,2,1,0:T(8,128)(2,1)S(1)} async-done(((bf16[8,2,128,128]{3,2,1,0:T(8,128)(2,1)}), bf16[8,2,128,128]{3,2,1,0:T(8,128)(2,1)S(1)}, u32[]{:S(2)}, u32[]{:S(2)}) %all-to-all-start.1) | async-done | bytes 524320 | tf_op jit(solution)/shard_map/all_to_all | solution.py:87
  30.7 11.3 %gather_fusion.1 = bf16[384,128,128]{2,1,0:T(8,128)(2,1)} fusion(bf16[52,128,128]{2,1,0:T(8,128)(2,1)S(1)} %pad_maximum_fusion, s32[1024]{0:T(1024)S(1)} %pad_clamp_fusion), kind=kCustom, calls=%fused_computation.1 | custom fusion | bytes 25167360 | tf_op jit(solution)/shard_map/gather | solution.py:95
  42.0 11.6 %bitcast_convert_fusion.1 = bf16[24,128,128]{1,2,0:T(8,128)(2,1)S(1)} fusion(bf16[24,16,128,128]{3,2,1,0:T(8,128)(2,1)} %param.14, bf16[24,16,128,128]{3,2,1,0:T(8,128)(2,1)} %bitcast.90), kind=kOutput, calls=%fused_computation.14 | convolution fusion | flops 1611005952 | bytes 25952256 | tf_op jit(solution)/shard_map/rkab,rkbc->rac/dot_general | solution.py:96
  53.8 22.5 %all_to_all.94 = bf16[4,768,128]{1,2,0:T(8,128)(2,1)S(1)} all-to-all(bf16[4,768,128]{1,2,0:T(8,128)(2,1)S(1)} %copy.52), channel_id=1, replica_groups=mesh['mesh'=8,'state'=4] {'state'}, dimensions={0} | all-to-all | bytes 1572864 | tf_op jit(solution)/shard_map/all_to_all | solution.py:104
  76.4 2.4 convolution_convert_fusion.1
  79.2 21.5 %all_to_all.95 = bf16[768,4,128]{2,0,1:T(8,128)(2,1)S(1)} all-to-all(bf16[768,4,128]{2,0,1:T(8,128)(2,1)S(1)} %copy.53), channel_id=1, replica_groups=mesh['mesh'=8,'state'=4] {'state'}, dimensions={1} | all-to-all | bytes 1572864 | tf_op jit(solution)/shard_map/all_to_all | solution.py:112
  100.7 16.3 %fusion.14 = f32[24,128,16,128]{3,1,2,0:T(8,128)} fusion(bf16[24,128,128,1]{2,1,3,0:T(8,128)(2,1)S(1)} %bitcast.95, bf16[24,16,128,128]{3,2,1,0:T(8,128)(2,1)} %param.14), kind=kOutput, calls=%fused_computation.62 | convolution fusion | flops 1610612736 | bytes 38535168 | tf_op jit(solution)/shard_map/rkab,rac->rkbc/dot_general | solution.py:114
  117.1 24.7 %copy.55 = f32[384,128,128]{2,1,0:T(8,128)} copy(f32[384,128,128]{1,2,0:T(8,128)} %bitcast.87) | data formatting | bytes 50331648 | tf_op jit(solution)/shard_map/reshape | solution.py:118
  141.7 2.2 broadcast.426.clone
  144.0 79.5 %scatter_fusion = f32[52,128,128]{2,1,0:T(8,128)} fusion(f32[52,128,128]{2,1,0:T(8,128)} %broadcast.426.clone, s32[384]{0:T(512)S(1)} %get-tuple-element.51, f32[384,128,128]{2,1,0:T(8,128)} %copy.55), kind=kCustom, calls=%fused_computation.4 | custom fusion | flops 6291456 | bytes 75499008 | tf_op jit(solution)/shard_map/scatter-add | solution.py:117
  223.5 2.2 convert.14
  226.6 5.2 %all-to-all-start.4 = ((bf16[8,2,128,128]{3,2,1,0:T(8,128)(2,1)}), bf16[8,2,128,128]{3,2,1,0:T(8,128)(2,1)}, u32[]{:S(2)}, u32[]{:S(2)}) async-start(bf16[8,2,128,128]{3,2,1,0:T(8,128)(2,1)} %bitcast.20), calls=%async_computation.4 | async-start | bytes 1048576 | tf_op jit(solution)/shard_map/all_to_all | solution.py:130
  234.9 2.2 collective-permute-start.3
  237.1 5.1 %all-to-all-done.4 = bf16[8,2,128,128]{3,2,1,0:T(8,128)(2,1)} async-done(((bf16[8,2,128,128]{3,2,1,0:T(8,128)(2,1)}), bf16[8,2,128,128]{3,2,1,0:T(8,128)(2,1)}, u32[]{:S(2)}, u32[]{:S(2)}) %all-to-all-start.4) | async-done | bytes 524320 | tf_op jit(solution)/shard_map/all_to_all | solution.py:130
  247.8 2.6 collective-permute-start.5
  251.9 3.7 all-to-all-start.5
  257.0 8.0 %all-to-all-done.5 = bf16[8,2,128,128]{3,2,1,0:T(8,128)(2,1)S(1)} async-done(((bf16[8,2,128,128]{3,2,1,0:T(8,128)(2,1)}), bf16[8,2,128,128]{3,2,1,0:T(8,128)(2,1)S(1)}, u32[]{:S(2)}, u32[]{:S(2)}) %all-to-all-start.5) | async-done | bytes 524320 | tf_op jit(solution)/shard_map/all_to_all | solution.py:87
  266.5 11.3 %gather_fusion.3 = bf16[384,128,128]{2,1,0:T(8,128)(2,1)} fusion(bf16[52,128,128]{2,1,0:T(8,128)(2,1)S(1)} %pad_maximum_fusion.1, s32[1024]{0:T(1024)S(1)} %pad_clamp_fusion), kind=kCustom, calls=%fused_computation.3 | custom fusion | bytes 25167360 | tf_op jit(solution)/shard_map/gather | solution.py:95
  277.8 11.6 %bitcast_convert_fusion = bf16[24,128,128]{1,2,0:T(8,128)(2,1)S(1)} fusion(bf16[24,16,128,128]{3,2,1,0:T(8,128)(2,1)} %param.14, bf16[24,16,128,128]{3,2,1,0:T(8,128)(2,1)} %bitcast.89), kind=kOutput, calls=%fused_computation.11 | convolution fusion | flops 1611005952 | bytes 25952256 | tf_op jit(solution)/shard_map/rkab,rkbc->rac/dot_general | solution.py:96
  289.6 20.5 %all_to_all.96 = bf16[4,768,128]{1,2,0:T(8,128)(2,1)S(1)} all-to-all(bf16[4,768,128]{1,2,0:T(8,128)(2,1)S(1)} %copy.56), channel_id=1, replica_groups=mesh['mesh'=8,'state'=4] {'state'}, dimensions={0} | all-to-all | bytes 1572864 | tf_op jit(solution)/shard_map/all_to_all | solution.py:104
  313.8 21.5 %all_to_all.97 = bf16[768,4,128]{2,0,1:T(8,128)(2,1)S(1)} all-to-all(bf16[768,4,128]{2,0,1:T(8,128)(2,1)S(1)} %copy.57), channel_id=1, replica_groups=mesh['mesh'=8,'state'=4] {'state'}, dimensions={1} | all-to-all | bytes 1572864 | tf_op jit(solution)/shard_map/all_to_all | solution.py:112
  335.3 16.3 %fusion.15 = f32[24,128,16,128]{3,1,2,0:T(8,128)} fusion(bf16[24,128,128,1]{2,1,3,0:T(8,128)(2,1)S(1)} %bitcast.96, bf16[24,16,128,128]{3,2,1,0:T(8,128)(2,1)} %param.14), kind=kOutput, calls=%fused_computation.63 | convolution fusion | flops 1610612736 | bytes 38535168 | tf_op jit(solution)/shard_map/rkab,rac->rkbc/dot_general | solution.py:114
  351.6 24.7 %copy.59 = f32[384,128,128]{2,1,0:T(8,128)} copy(f32[384,128,128]{1,2,0:T(8,128)} %bitcast.88) | data formatting | bytes 50331648 | tf_op jit(solution)/shard_map/reshape | solution.py:118
  376.3 2.2 broadcast.426
  378.5 79.5 %scatter_fusion.2 = f32[52,128,128]{2,1,0:T(8,128)} fusion(f32[52,128,128]{2,1,0:T(8,128)} %broadcast.426, s32[384]{0:T(512)S(1)} %get-tuple-element.51, f32[384,128,128]{2,1,0:T(8,128)} %copy.59), kind=kCustom, calls=%fused_computation.6 | custom fusion | flops 6291456 | bytes 75499008 | tf_op jit(solution)/shard_map/scatter-add | solution.py:117
  458.0 2.2 convert.15
  461.1 5.2 %all-to-all-start.8 = ((bf16[8,2,128,128]{3,2,1,0:T(8,128)(2,1)}), bf16[8,2,128,128]{3,2,1,0:T(8,128)(2,1)}, u32[]{:S(2)}, u32[]{:S(2)}) async-start(bf16[8,2,128,128]{3,2,1,0:T(8,128)(2,1)} %bitcast.41), calls=%async_computation.8 | async-start | bytes 1048576 | tf_op jit(solution)/shard_map/all_to_all | solution.py:130
  468.2 2.2 collective-permute-start.7
  470.4 6.3 %all-to-all-done.8 = bf16[8,2,128,128]{3,2,1,0:T(8,128)(2,1)} async-done(((bf16[8,2,128,128]{3,2,1,0:T(8,128)(2,1)}), bf16[8,2,128,128]{3,2,1,0:T(8,128)(2,1)}, u32[]{:S(2)}, u32[]{:S(2)}) %all-to-all-start.8) | async-done | bytes 524320 | tf_op jit(solution)/shard_map/all_to_all | solution.py:130
  (91 shorter events, 37.1 us)
Async XLA Ops:
  0.6 75.8 %copy-start = (bf16[512,512]{1,0:T(8,128)(2,1)S(1)}, bf16[512,512]{1,0:T(8,128)(2,1)}, u32[]{:S(2)}) copy-start(bf16[512,512]{1,0:T(8,128)(2,1)} %param.16) | copy-start | bytes 1572868
  3.9 9.9 %all-to-all-start = ((s32[8,1,2]{2,1,0:T(1,128)}), s32[8,1,2]{2,1,0:T(1,128)S(1)}, u32[]{:S(2)}, u32[]{:S(2)}) async-start(s32[8,1,2]{2,1,0:T(1,128)} %copy.49), calls=%async_computation | async-start | bytes 8192 | tf_op jit(solution)/shard_map/all_to_all | solution.py:72
  10.7 8.4 %collective-permute-start = (bf16[768,128]{1,0:T(8,128)(2,1)S(1)}, bf16[768,128]{1,0:T(8,128)(2,1)S(1)}, u32[]{:S(2)}, u32[]{:S(2)}) collective-permute-start(bf16[768,128]{1,0:T(8,128)(2,1)S(1)} %get-tuple-element.60), channel_id=1, source_target_pairs={{0,4},{4,8},{8,12},{12,16},{16,20},{20,24},{24,28},{28,0},{1,5},{5... | collective-permute-start | bytes 589832 | tf_op jit(solution)/shard_map/ppermute | solution.py:18
  11.2 7.8 %collective-permute-start.1 = (bf16[768,128]{1,0:T(8,128)(2,1)S(1)}, bf16[768,128]{1,0:T(8,128)(2,1)S(1)}, u32[]{:S(2)}, u32[]{:S(2)}) collective-permute-start(bf16[768,128]{1,0:T(8,128)(2,1)S(1)} %get-tuple-element.61), channel_id=1, source_target_pairs={{4,0},{8,4},{12,8},{16,12},{20,16},{24,20},{28,24},{0,28},{5,1},{9... | collective-permute-start | bytes 589832 | tf_op jit(solution)/shard_map/ppermute | solution.py:20
  15.5 13.2 %all-to-all-start.1 = ((bf16[8,2,128,128]{3,2,1,0:T(8,128)(2,1)}), bf16[8,2,128,128]{3,2,1,0:T(8,128)(2,1)S(1)}, u32[]{:S(2)}, u32[]{:S(2)}) async-start(bf16[8,2,128,128]{3,2,1,0:T(8,128)(2,1)} %bitcast.4), calls=%async_computation.1 | async-start | bytes 1048576 | tf_op jit(solution)/shard_map/all_to_all | solution.py:87
  28.7 0.8 copy-start.5
  225.7 7.3 %copy-start.1 = (bf16[52,128,128]{2,1,0:T(8,128)(2,1)}, bf16[52,128,128]{2,1,0:T(8,128)(2,1)S(1)}, u32[]{:S(2)}) copy-start(bf16[52,128,128]{2,1,0:T(8,128)(2,1)S(1)} %convert.14) | copy-start | bytes 5111812
  226.6 15.6 %all-to-all-start.4 = ((bf16[8,2,128,128]{3,2,1,0:T(8,128)(2,1)}), bf16[8,2,128,128]{3,2,1,0:T(8,128)(2,1)}, u32[]{:S(2)}, u32[]{:S(2)}) async-start(bf16[8,2,128,128]{3,2,1,0:T(8,128)(2,1)} %bitcast.20), calls=%async_computation.4 | async-start | bytes 1048576 | tf_op jit(solution)/shard_map/all_to_all | solution.py:130
  234.4 10.9 %collective-permute-start.2 = (bf16[6,128,128]{2,1,0:T(8,128)(2,1)S(1)}, bf16[6,128,128]{2,1,0:T(8,128)(2,1)}, u32[]{:S(2)}, u32[]{:S(2)}) collective-permute-start(bf16[6,128,128]{2,1,0:T(8,128)(2,1)S(1)} %get-tuple-element.57), channel_id=1, source_target_pairs={{0,4},{4,8},{8,12},{12,16},{16,20},{20,24},{24,28},{28,0},{1,5},{5... | collective-permute-start | bytes 589832 | tf_op jit(solution)/shard_map/ppermute | solution.py:30
  234.9 11.5 %collective-permute-start.3 = (bf16[6,128,128]{2,1,0:T(8,128)(2,1)S(1)}, bf16[6,128,128]{2,1,0:T(8,128)(2,1)}, u32[]{:S(2)}, u32[]{:S(2)}) collective-permute-start(bf16[6,128,128]{2,1,0:T(8,128)(2,1)S(1)} %get-tuple-element.56), channel_id=1, source_target_pairs={{0,28},{4,0},{8,4},{12,8},{16,12},{20,16},{24,20},{28,24},{1,29},{... | collective-permute-start | bytes 589832 | tf_op jit(solution)/shard_map/ppermute | solution.py:30
  244.9 2.5 copy-start.3
  247.8 8.1 %collective-permute-start.4 = (bf16[768,128]{1,0:T(8,128)(2,1)S(1)}, bf16[768,128]{1,0:T(8,128)(2,1)S(1)}, u32[]{:S(2)}, u32[]{:S(2)}) collective-permute-start(bf16[768,128]{1,0:T(8,128)(2,1)S(1)} %get-tuple-element.58), channel_id=1, source_target_pairs={{0,4},{4,8},{8,12},{12,16},{16,20},{20,24},{24,28},{28,0},{1,5},{5... | collective-permute-start | bytes 589832 | tf_op jit(solution)/shard_map/ppermute | solution.py:18
  247.8 8.0 %collective-permute-start.5 = (bf16[768,128]{1,0:T(8,128)(2,1)S(1)}, bf16[768,128]{1,0:T(8,128)(2,1)S(1)}, u32[]{:S(2)}, u32[]{:S(2)}) collective-permute-start(bf16[768,128]{1,0:T(8,128)(2,1)S(1)} %get-tuple-element.59), channel_id=1, source_target_pairs={{4,0},{8,4},{12,8},{16,12},{20,16},{24,20},{28,24},{0,28},{5,1},{9... | collective-permute-start | bytes 589832 | tf_op jit(solution)/shard_map/ppermute | solution.py:20
  251.9 13.2 %all-to-all-start.5 = ((bf16[8,2,128,128]{3,2,1,0:T(8,128)(2,1)}), bf16[8,2,128,128]{3,2,1,0:T(8,128)(2,1)S(1)}, u32[]{:S(2)}, u32[]{:S(2)}) async-start(bf16[8,2,128,128]{3,2,1,0:T(8,128)(2,1)} %bitcast.25), calls=%async_computation.5 | async-start | bytes 1048576 | tf_op jit(solution)/shard_map/all_to_all | solution.py:87
  312.2 1.1 copy-start.6
  460.3 6.1 %copy-start.2 = (bf16[52,128,128]{2,1,0:T(8,128)(2,1)}, bf16[52,128,128]{2,1,0:T(8,128)(2,1)S(1)}, u32[]{:S(2)}) copy-start(bf16[52,128,128]{2,1,0:T(8,128)(2,1)S(1)} %convert.15) | copy-start | bytes 5111812
  461.1 15.6 %all-to-all-start.8 = ((bf16[8,2,128,128]{3,2,1,0:T(8,128)(2,1)}), bf16[8,2,128,128]{3,2,1,0:T(8,128)(2,1)}, u32[]{:S(2)}, u32[]{:S(2)}) async-start(bf16[8,2,128,128]{3,2,1,0:T(8,128)(2,1)} %bitcast.41), calls=%async_computation.8 | async-start | bytes 1048576 | tf_op jit(solution)/shard_map/all_to_all | solution.py:130
  467.6 12.2 %collective-permute-start.6 = (bf16[6,128,128]{2,1,0:T(8,128)(2,1)S(1)}, bf16[6,128,128]{2,1,0:T(8,128)(2,1)}, u32[]{:S(2)}, u32[]{:S(2)}) collective-permute-start(bf16[6,128,128]{2,1,0:T(8,128)(2,1)S(1)} %get-tuple-element.55), channel_id=1, source_target_pairs={{0,4},{4,8},{8,12},{12,16},{16,20},{20,24},{24,28},{28,0},{1,5},{5... | collective-permute-start | bytes 589832 | tf_op jit(solution)/shard_map/ppermute | solution.py:30
  468.2 12.8 %collective-permute-start.7 = (bf16[6,128,128]{2,1,0:T(8,128)(2,1)S(1)}, bf16[6,128,128]{2,1,0:T(8,128)(2,1)}, u32[]{:S(2)}, u32[]{:S(2)}) collective-permute-start(bf16[6,128,128]{2,1,0:T(8,128)(2,1)S(1)} %get-tuple-element.54), channel_id=1, source_target_pairs={{0,28},{4,0},{8,4},{12,8},{16,12},{20,16},{24,20},{28,24},{1,29},{... | collective-permute-start | bytes 589832 | tf_op jit(solution)/shard_map/ppermute | solution.py:30
  479.5 2.5 copy-start.4
where the time goes:
time: 487 us; the launch traced here: 484 us
  other arithmetic  184 us (38%)
  local copies, waits for them, and re-layouts  88.1 us (18%)
  blocking collectives  86.1 us (18%)
  matrix products  61 us (13%)
  starting transfers between devices  33.8 us (7%)
  waiting for transfers between devices  29.9 us (6%)
    scatter-add x2, other arithmetic, per_device(): jax.ops.segment_sum(spread.reshape(-1, block_size, state_cols), sources,...  159 us
    reshape x2, local copies, waits for them, and re-layouts, per_device(): spread.reshape(-1, block_size, state_cols)  49.3 us
    all_to_all x2, blocking collectives, per_device(): lax.all_to_all(pieces, 'state', split_axis=0, concat_axis=2, tiled=True)  43.1 us
    all_to_all x2, blocking collectives, per_device(): lax.all_to_all(back_rows, 'state', split_axis=1, concat_axis=0, tiled=True)  43 us
    dot_general x2, matrix products, per_device(): jnp.einsum('rkab,rac->rkbc', kern_blocks, returned, preferred_element_typ...  32.7 us
    dot_general x2, matrix products, per_device(): jnp.einsum('rkab,rkbc->rac', kern_blocks, picked, preferred_element_type=...  23.2 us
    gather x2, local copies, waits for them, and re-layouts, per_device(): picked = table[sources].reshape(block_rows, degree, block_size, state_cols)  22.6 us
    all_to_all x2, waiting for transfers between devices, per_device(): lax.all_to_all(blocks[asked], 'mesh', split_axis=0, concat_axis=0, tiled=...  17.6 us
  transfers between devices with their start and end apart: 13, of which 7 were waited for; matrix products, arithmetic and copies ran while one was open for 4% of the time, Pallas kernels for 0%

commit v1 on v0

--- a/solution.py
+++ b/solution.py
@@ -109,7 +109,12 @@
         back_rows = jnp.dot(
             potential_u.astype(jnp.bfloat16), state_kernel, preferred_element_type=jnp.float32
         ).astype(jnp.bfloat16)
-        returned = lax.all_to_all(back_rows, "state", split_axis=1, concat_axis=0, tiled=True)
+        returned = jnp.concatenate(
+            lax.all_to_all(
+                jnp.stack(jnp.split(back_rows, lax.axis_size("state"), axis=1)), "state", 0, 0
+            ),
+            axis=0,
+        )
         returned = returned.reshape(block_rows, block_size, state_cols)
         spread = jnp.einsum(
             "rkab,rac->rkbc", kern_blocks, returned, preferred_element_type=jnp.float32

time: 487 us -> 486 us (level)
  no operation moved by 1% of the time
where the time goes in v1:
time: 486 us; the launch traced here: 482 us
  other arithmetic  184 us (38%)
  local copies, waits for them, and re-layouts  87.5 us (18%)
  blocking collectives  86.1 us (18%)
  matrix products  60.9 us (13%)
  starting transfers between devices  33 us (7%)
  waiting for transfers between devices  29.9 us (6%)
    scatter-add x2, other arithmetic, per_device(): jax.ops.segment_sum(spread.reshape(-1, block_size, state_cols), sources,...  159 us
    reshape x2, local copies, waits for them, and re-layouts, per_device(): spread.reshape(-1, block_size, state_cols)  49.3 us
    all_to_all x2, blocking collectives, per_device(): lax.all_to_all(pieces, 'state', split_axis=0, concat_axis=2, tiled=True)  43.1 us
    all_to_all x2, blocking collectives, per_device(): lax.all_to_all(jnp.stack(jnp.split(back_rows, lax.axis_size('state'), axi...  43 us
    dot_general x2, matrix products, per_device(): jnp.einsum('rkab,rac->rkbc', kern_blocks, returned, preferred_element_typ...  32.7 us
    dot_general x2, matrix products, per_device(): jnp.einsum('rkab,rkbc->rac', kern_blocks, picked, preferred_element_type=...  23.2 us
    gather x2, local copies, waits for them, and re-layouts, per_device(): picked = table[sources].reshape(block_rows, degree, block_size, state_cols)  22.6 us
    all_to_all x2, waiting for transfers between devices, per_device(): lax.all_to_all(blocks[asked], 'mesh', split_axis=0, concat_axis=0, tiled=...  17.6 us
  transfers between devices with their start and end apart: 13, of which 7 were waited for; matrix products, arithmetic and copies ran while one was open for 4% of the time, Pallas kernels for 0%

profile of v1, /device:TPU:0, one launch (start us, length us, event | category | flops | bytes accessed | tf_op | source)
XLA Modules:
  0.0 482.5 jit_solution(12345297492549750532)
XLA Ops:
  3.9 5.2 %all-to-all-start = ((s32[8,1,2]{2,1,0:T(1,128)}), s32[8,1,2]{2,1,0:T(1,128)S(1)}, u32[]{:S(2)}, u32[]{:S(2)}) async-start(s32[8,1,2]{2,1,0:T(1,128)} %copy.47), calls=%async_computation | async-start | bytes 8192 | tf_op jit(solution)/shard_map/all_to_all | solution.py:72
  11.2 2.2 collective-permute-start.1
  15.5 3.5 all-to-all-start.1
  19.1 9.5 %all-to-all-done.1 = bf16[8,2,128,128]{3,2,1,0:T(8,128)(2,1)S(1)} async-done(((bf16[8,2,128,128]{3,2,1,0:T(8,128)(2,1)}), bf16[8,2,128,128]{3,2,1,0:T(8,128)(2,1)S(1)}, u32[]{:S(2)}, u32[]{:S(2)}) %all-to-all-start.1) | async-done | bytes 524320 | tf_op jit(solution)/shard_map/all_to_all | solution.py:87
  30.7 11.3 %gather_fusion.1 = bf16[384,128,128]{2,1,0:T(8,128)(2,1)} fusion(bf16[52,128,128]{2,1,0:T(8,128)(2,1)S(1)} %pad_maximum_fusion, s32[1024]{0:T(1024)S(1)} %pad_clamp_fusion), kind=kCustom, calls=%fused_computation.1 | custom fusion | bytes 25167360 | tf_op jit(solution)/shard_map/gather | solution.py:95
  42.0 11.6 %bitcast_convert_fusion.1 = bf16[24,128,128]{1,2,0:T(8,128)(2,1)S(1)} fusion(bf16[24,16,128,128]{3,2,1,0:T(8,128)(2,1)} %param.14, bf16[24,16,128,128]{3,2,1,0:T(8,128)(2,1)} %bitcast.100), kind=kOutput, calls=%fused_computation.14 | convolution fusion | flops 1611005952 | bytes 25952256 | tf_op jit(solution)/shard_map/rkab,rkbc->rac/dot_general | solution.py:96
  53.9 22.5 %all_to_all.72 = bf16[4,768,128]{1,2,0:T(8,128)(2,1)S(1)} all-to-all(bf16[4,768,128]{1,2,0:T(8,128)(2,1)S(1)} %copy.50), channel_id=1, replica_groups=mesh['mesh'=8,'state'=4] {'state'}, dimensions={0} | all-to-all | bytes 1572864 | tf_op jit(solution)/shard_map/all_to_all | solution.py:104
  76.4 2.5 convolution_convert_fusion.1
  79.1 21.5 %all_to_all.73 = bf16[4,768,128]{2,1,0:T(8,128)(2,1)S(1)} all-to-all(bf16[4,768,128]{2,1,0:T(8,128)(2,1)S(1)} %pad_maximum_fusion.4), channel_id=1, replica_groups=mesh['mesh'=8,'state'=4] {'state'}, dimensions={0} | all-to-all | bytes 1572864 | tf_op jit(solution)/shard_map/all_to_all | solution.py:113
  100.6 16.3 %fusion.14 = f32[24,128,16,128]{3,1,2,0:T(8,128)} fusion(bf16[24,128,128,1]{2,1,3,0:T(8,128)(2,1)S(1)} %bitcast.105, bf16[24,16,128,128]{3,2,1,0:T(8,128)(2,1)} %param.14), kind=kOutput, calls=%fused_computation.72 | convolution fusion | flops 1610612736 | bytes 38535168 | tf_op jit(solution)/shard_map/rkab,rac->rkbc/dot_general | solution.py:119
  117.0 24.7 %copy.52 = f32[384,128,128]{2,1,0:T(8,128)} copy(f32[384,128,128]{1,2,0:T(8,128)} %bitcast.97) | data formatting | bytes 50331648 | tf_op jit(solution)/shard_map/reshape | solution.py:123
  141.6 2.2 broadcast.426.clone
  143.8 79.6 %scatter_fusion = f32[52,128,128]{2,1,0:T(8,128)} fusion(f32[52,128,128]{2,1,0:T(8,128)} %broadcast.426.clone, s32[384]{0:T(512)S(1)} %get-tuple-element.51, f32[384,128,128]{2,1,0:T(8,128)} %copy.52), kind=kCustom, calls=%fused_computation.4 | custom fusion | flops 6291456 | bytes 75499008 | tf_op jit(solution)/shard_map/scatter-add | solution.py:122
  223.4 2.2 convert.14
  226.6 4.8 all-to-all-start.4
  234.4 2.2 collective-permute-start.3
  236.6 5.1 %all-to-all-done.4 = bf16[8,2,128,128]{3,2,1,0:T(8,128)(2,1)} async-done(((bf16[8,2,128,128]{3,2,1,0:T(8,128)(2,1)}), bf16[8,2,128,128]{3,2,1,0:T(8,128)(2,1)}, u32[]{:S(2)}, u32[]{:S(2)}) %all-to-all-start.4) | async-done | bytes 524320 | tf_op jit(solution)/shard_map/all_to_all | solution.py:135
  247.4 2.6 collective-permute-start.5
  251.4 3.7 all-to-all-start.5
  256.5 8.0 %all-to-all-done.5 = bf16[8,2,128,128]{3,2,1,0:T(8,128)(2,1)S(1)} async-done(((bf16[8,2,128,128]{3,2,1,0:T(8,128)(2,1)}), bf16[8,2,128,128]{3,2,1,0:T(8,128)(2,1)S(1)}, u32[]{:S(2)}, u32[]{:S(2)}) %all-to-all-start.5) | async-done | bytes 524320 | tf_op jit(solution)/shard_map/all_to_all | solution.py:87
  266.0 11.3 %gather_fusion.3 = bf16[384,128,128]{2,1,0:T(8,128)(2,1)} fusion(bf16[52,128,128]{2,1,0:T(8,128)(2,1)S(1)} %pad_maximum_fusion.1, s32[1024]{0:T(1024)S(1)} %pad_clamp_fusion), kind=kCustom, calls=%fused_computation.3 | custom fusion | bytes 25167360 | tf_op jit(solution)/shard_map/gather | solution.py:95
  277.3 11.6 %bitcast_convert_fusion = bf16[24,128,128]{1,2,0:T(8,128)(2,1)S(1)} fusion(bf16[24,16,128,128]{3,2,1,0:T(8,128)(2,1)} %param.14, bf16[24,16,128,128]{3,2,1,0:T(8,128)(2,1)} %bitcast.99), kind=kOutput, calls=%fused_computation.11 | convolution fusion | flops 1611005952 | bytes 25952256 | tf_op jit(solution)/shard_map/rkab,rkbc->rac/dot_general | solution.py:96
  289.2 20.5 %all_to_all.74 = bf16[4,768,128]{1,2,0:T(8,128)(2,1)S(1)} all-to-all(bf16[4,768,128]{1,2,0:T(8,128)(2,1)S(1)} %copy.53), channel_id=1, replica_groups=mesh['mesh'=8,'state'=4] {'state'}, dimensions={0} | all-to-all | bytes 1572864 | tf_op jit(solution)/shard_map/all_to_all | solution.py:104
  313.0 21.5 %all_to_all.75 = bf16[4,768,128]{2,1,0:T(8,128)(2,1)S(1)} all-to-all(bf16[4,768,128]{2,1,0:T(8,128)(2,1)S(1)} %pad_maximum_fusion.5), channel_id=1, replica_groups=mesh['mesh'=8,'state'=4] {'state'}, dimensions={0} | all-to-all | bytes 1572864 | tf_op jit(solution)/shard_map/all_to_all | solution.py:113
  334.5 16.3 %fusion.15 = f32[24,128,16,128]{3,1,2,0:T(8,128)} fusion(bf16[24,128,128,1]{2,1,3,0:T(8,128)(2,1)S(1)} %bitcast.106, bf16[24,16,128,128]{3,2,1,0:T(8,128)(2,1)} %param.14), kind=kOutput, calls=%fused_computation.73 | convolution fusion | flops 1610612736 | bytes 38535168 | tf_op jit(solution)/shard_map/rkab,rac->rkbc/dot_general | solution.py:119
  350.9 24.7 %copy.55 = f32[384,128,128]{2,1,0:T(8,128)} copy(f32[384,128,128]{1,2,0:T(8,128)} %bitcast.98) | data formatting | bytes 50331648 | tf_op jit(solution)/shard_map/reshape | solution.py:123
  375.5 2.2 broadcast.426
  377.7 79.6 %scatter_fusion.2 = f32[52,128,128]{2,1,0:T(8,128)} fusion(f32[52,128,128]{2,1,0:T(8,128)} %broadcast.426, s32[384]{0:T(512)S(1)} %get-tuple-element.51, f32[384,128,128]{2,1,0:T(8,128)} %copy.55), kind=kCustom, calls=%fused_computation.6 | custom fusion | flops 6291456 | bytes 75499008 | tf_op jit(solution)/shard_map/scatter-add | solution.py:122
  457.3 2.2 convert.15
  460.5 4.9 %all-to-all-start.8 = ((bf16[8,2,128,128]{3,2,1,0:T(8,128)(2,1)}), bf16[8,2,128,128]{3,2,1,0:T(8,128)(2,1)}, u32[]{:S(2)}, u32[]{:S(2)}) async-start(bf16[8,2,128,128]{3,2,1,0:T(8,128)(2,1)} %bitcast.45), calls=%async_computation.8 | async-start | bytes 1048576 | tf_op jit(solution)/shard_map/all_to_all | solution.py:135
  467.2 2.2 collective-permute-start.7
  469.4 6.3 %all-to-all-done.8 = bf16[8,2,128,128]{3,2,1,0:T(8,128)(2,1)} async-done(((bf16[8,2,128,128]{3,2,1,0:T(8,128)(2,1)}), bf16[8,2,128,128]{3,2,1,0:T(8,128)(2,1)}, u32[]{:S(2)}, u32[]{:S(2)}) %all-to-all-start.8) | async-done | bytes 524320 | tf_op jit(solution)/shard_map/all_to_all | solution.py:135
  (93 shorter events, 36.7 us)
Async XLA Ops:
  0.6 75.8 %copy-start = (bf16[512,512]{1,0:T(8,128)(2,1)S(1)}, bf16[512,512]{1,0:T(8,128)(2,1)}, u32[]{:S(2)}) copy-start(bf16[512,512]{1,0:T(8,128)(2,1)} %param.16) | copy-start | bytes 1572868
  3.9 9.9 %all-to-all-start = ((s32[8,1,2]{2,1,0:T(1,128)}), s32[8,1,2]{2,1,0:T(1,128)S(1)}, u32[]{:S(2)}, u32[]{:S(2)}) async-start(s32[8,1,2]{2,1,0:T(1,128)} %copy.47), calls=%async_computation | async-start | bytes 8192 | tf_op jit(solution)/shard_map/all_to_all | solution.py:72
  10.7 8.4 %collective-permute-start = (bf16[768,128]{1,0:T(8,128)(2,1)S(1)}, bf16[768,128]{1,0:T(8,128)(2,1)S(1)}, u32[]{:S(2)}, u32[]{:S(2)}) collective-permute-start(bf16[768,128]{1,0:T(8,128)(2,1)S(1)} %get-tuple-element.68), channel_id=1, source_target_pairs={{0,4},{4,8},{8,12},{12,16},{16,20},{20,24},{24,28},{28,0},{1,5},{5... | collective-permute-start | bytes 589832 | tf_op jit(solution)/shard_map/ppermute | solution.py:18
  11.2 7.8 %collective-permute-start.1 = (bf16[768,128]{1,0:T(8,128)(2,1)S(1)}, bf16[768,128]{1,0:T(8,128)(2,1)S(1)}, u32[]{:S(2)}, u32[]{:S(2)}) collective-permute-start(bf16[768,128]{1,0:T(8,128)(2,1)S(1)} %get-tuple-element.69), channel_id=1, source_target_pairs={{4,0},{8,4},{12,8},{16,12},{20,16},{24,20},{28,24},{0,28},{5,1},{9... | collective-permute-start | bytes 589832 | tf_op jit(solution)/shard_map/ppermute | solution.py:20
  15.5 13.2 %all-to-all-start.1 = ((bf16[8,2,128,128]{3,2,1,0:T(8,128)(2,1)}), bf16[8,2,128,128]{3,2,1,0:T(8,128)(2,1)S(1)}, u32[]{:S(2)}, u32[]{:S(2)}) async-start(bf16[8,2,128,128]{3,2,1,0:T(8,128)(2,1)} %bitcast.4), calls=%async_computation.1 | async-start | bytes 1048576 | tf_op jit(solution)/shard_map/all_to_all | solution.py:87
  28.7 0.8 copy-start.5
  225.7 6.9 %copy-start.1 = (bf16[52,128,128]{2,1,0:T(8,128)(2,1)}, bf16[52,128,128]{2,1,0:T(8,128)(2,1)S(1)}, u32[]{:S(2)}) copy-start(bf16[52,128,128]{2,1,0:T(8,128)(2,1)S(1)} %convert.14) | copy-start | bytes 5111812
  226.6 15.2 %all-to-all-start.4 = ((bf16[8,2,128,128]{3,2,1,0:T(8,128)(2,1)}), bf16[8,2,128,128]{3,2,1,0:T(8,128)(2,1)}, u32[]{:S(2)}, u32[]{:S(2)}) async-start(bf16[8,2,128,128]{3,2,1,0:T(8,128)(2,1)} %bitcast.22), calls=%async_computation.4 | async-start | bytes 1048576 | tf_op jit(solution)/shard_map/all_to_all | solution.py:135
  233.9 10.9 %collective-permute-start.2 = (bf16[6,128,128]{2,1,0:T(8,128)(2,1)S(1)}, bf16[6,128,128]{2,1,0:T(8,128)(2,1)}, u32[]{:S(2)}, u32[]{:S(2)}) collective-permute-start(bf16[6,128,128]{2,1,0:T(8,128)(2,1)S(1)} %get-tuple-element.57), channel_id=1, source_target_pairs={{0,4},{4,8},{8,12},{12,16},{16,20},{20,24},{24,28},{28,0},{1,5},{5... | collective-permute-start | bytes 589832 | tf_op jit(solution)/shard_map/ppermute | solution.py:30
  234.4 11.5 %collective-permute-start.3 = (bf16[6,128,128]{2,1,0:T(8,128)(2,1)S(1)}, bf16[6,128,128]{2,1,0:T(8,128)(2,1)}, u32[]{:S(2)}, u32[]{:S(2)}) collective-permute-start(bf16[6,128,128]{2,1,0:T(8,128)(2,1)S(1)} %get-tuple-element.56), channel_id=1, source_target_pairs={{0,28},{4,0},{8,4},{12,8},{16,12},{20,16},{24,20},{28,24},{1,29},{... | collective-permute-start | bytes 589832 | tf_op jit(solution)/shard_map/ppermute | solution.py:30
  244.5 2.5 copy-start.3
  247.3 8.1 %collective-permute-start.4 = (bf16[768,128]{1,0:T(8,128)(2,1)S(1)}, bf16[768,128]{1,0:T(8,128)(2,1)S(1)}, u32[]{:S(2)}, u32[]{:S(2)}) collective-permute-start(bf16[768,128]{1,0:T(8,128)(2,1)S(1)} %get-tuple-element.62), channel_id=1, source_target_pairs={{0,4},{4,8},{8,12},{12,16},{16,20},{20,24},{24,28},{28,0},{1,5},{5... | collective-permute-start | bytes 589832 | tf_op jit(solution)/shard_map/ppermute | solution.py:18
  247.4 8.0 %collective-permute-start.5 = (bf16[768,128]{1,0:T(8,128)(2,1)S(1)}, bf16[768,128]{1,0:T(8,128)(2,1)S(1)}, u32[]{:S(2)}, u32[]{:S(2)}) collective-permute-start(bf16[768,128]{1,0:T(8,128)(2,1)S(1)} %get-tuple-element.63), channel_id=1, source_target_pairs={{4,0},{8,4},{12,8},{16,12},{20,16},{24,20},{28,24},{0,28},{5,1},{9... | collective-permute-start | bytes 589832 | tf_op jit(solution)/shard_map/ppermute | solution.py:20
  251.4 13.2 %all-to-all-start.5 = ((bf16[8,2,128,128]{3,2,1,0:T(8,128)(2,1)}), bf16[8,2,128,128]{3,2,1,0:T(8,128)(2,1)S(1)}, u32[]{:S(2)}, u32[]{:S(2)}) async-start(bf16[8,2,128,128]{3,2,1,0:T(8,128)(2,1)} %bitcast.27), calls=%async_computation.5 | async-start | bytes 1048576 | tf_op jit(solution)/shard_map/all_to_all | solution.py:87
  311.8 1.1 copy-start.6
  459.6 5.7 %copy-start.2 = (bf16[52,128,128]{2,1,0:T(8,128)(2,1)}, bf16[52,128,128]{2,1,0:T(8,128)(2,1)S(1)}, u32[]{:S(2)}) copy-start(bf16[52,128,128]{2,1,0:T(8,128)(2,1)S(1)} %convert.15) | copy-start | bytes 5111812
  460.5 15.2 %all-to-all-start.8 = ((bf16[8,2,128,128]{3,2,1,0:T(8,128)(2,1)}), bf16[8,2,128,128]{3,2,1,0:T(8,128)(2,1)}, u32[]{:S(2)}, u32[]{:S(2)}) async-start(bf16[8,2,128,128]{3,2,1,0:T(8,128)(2,1)} %bitcast.45), calls=%async_computation.8 | async-start | bytes 1048576 | tf_op jit(solution)/shard_map/all_to_all | solution.py:135
  466.6 12.2 %collective-permute-start.6 = (bf16[6,128,128]{2,1,0:T(8,128)(2,1)S(1)}, bf16[6,128,128]{2,1,0:T(8,128)(2,1)}, u32[]{:S(2)}, u32[]{:S(2)}) collective-permute-start(bf16[6,128,128]{2,1,0:T(8,128)(2,1)S(1)} %get-tuple-element.55), channel_id=1, source_target_pairs={{0,4},{4,8},{8,12},{12,16},{16,20},{20,24},{24,28},{28,0},{1,5},{5... | collective-permute-start | bytes 589832 | tf_op jit(solution)/shard_map/ppermute | solution.py:30
  467.2 12.8 %collective-permute-start.7 = (bf16[6,128,128]{2,1,0:T(8,128)(2,1)S(1)}, bf16[6,128,128]{2,1,0:T(8,128)(2,1)}, u32[]{:S(2)}, u32[]{:S(2)}) collective-permute-start(bf16[6,128,128]{2,1,0:T(8,128)(2,1)S(1)} %get-tuple-element.54), channel_id=1, source_target_pairs={{0,28},{4,0},{8,4},{12,8},{16,12},{20,16},{24,20},{28,24},{1,29},{... | collective-permute-start | bytes 589832 | tf_op jit(solution)/shard_map/ppermute | solution.py:30
  478.5 2.5 copy-start.4
